TPU v7x, 128 devices: a whole 4x4x4 slice. The times are simulated.
128 devices in a mesh: patch: 16 (over y, x), col: 8 (over z, core).
Axes of the slice: x: 4, y: 4, z: 4, core: 2. Of those that a mesh axis runs over, the one named last changes fastest.
Arguments:
- potential0: float32 [512, 16, 128], P(('patch', 'col')), may hold values from -3 to 3
- source_term: float32 [512, 16, 128], P(('patch', 'col')), may hold values from -9 to 9
- self_coef: float32 [512, 128], P(('patch', 'col')), may hold values from 1 to 4
- nearfield: float32 [512, 24, 128, 128], P(('patch', 'col')), may hold values from -0.109375 to 0.109375
- precond: float32 [512, 128, 128], P(('patch', 'col')), may hold values from -1 to 2
- exch_current: float32 [512, 128], P(('patch', 'col')), may hold values from 0.05 to 0.5
- conductance: float32 [512, 128], P(('patch', 'col')), may hold values from 0.1 to 1
- member: int32 [512, 128], P(('patch', 'col')), may hold values from 0 to 63
- anode_drive: float32 [64], replicated, may hold values from -1 to 1
- pair_source: int32 [512, 24], P(('patch', 'col')), may hold values from 0 to 39
- pair_count: int32 [512], P(('patch', 'col')), may hold values from 1 to 24, as said below
Outputs:
- potential: float32 [512, 16, 128], P(('patch', 'col'))
- residual: float32 [512, 16, 128], P(('patch', 'col'))
Inputs may be any that keep to these rules, and one draw needn't show every extreme that they name: Slots k < pair_count[b] of block b are live; some block has all 24 slots live, and the blocks of some devices hold far more live pairs than those of others.
All inputs are finite; a program needn't handle non-finite values.
Results may differ from a plain program's by a relative error of at most 0.0003.
Values sent between devices are 32-bit elements; how exact they have to be, the bound alone decides.
A program may use at most 64 MiB of HBM per device.

v0:
```python
import jax
import jax.numpy as jnp
from jax import lax
from jax.sharding import PartitionSpec as P

NEWTON = 2
GMRES = 2
ALPHA = 0.6
BETA = 0.4
EPS = 1e-06


def from_behind(array, axis, by):
    size = lax.axis_size(axis)
    return lax.ppermute(array, axis, [(i, (i + by) % size) for i in range(size)])


def column_sum(left, right):
    return jnp.sum(left * right, axis=(0, 2))


def least_squares(columns, beta):
    depth = len(columns)
    hessen = jnp.zeros((beta.shape[0], depth + 1, depth), jnp.float32)
    for place in range(depth):
        hessen = hessen.at[:, : place + 2, place].set(columns[place].T)
    gram = jnp.einsum("cij,cik->cjk", hessen, hessen, precision=lax.Precision.HIGHEST)
    right = beta[:, None] * hessen[:, 0, :]
    lower = jnp.linalg.cholesky(gram)
    middle = jax.scipy.linalg.solve_triangular(lower, right[:, :, None], lower=True)
    return jax.scipy.linalg.solve_triangular(lower, middle, lower=True, trans=1)[:, :, 0]


def body(
    potential0,
    source_term,
    self_coef,
    nearfield,
    precond,
    exch_current,
    conductance,
    member,
    anode_drive,
    pair_source,
    pair_count,
):
    pair_slots = pair_source.shape[1]
    live_mask = (jnp.arange(pair_slots, dtype=jnp.int32)[None, :] < pair_count[:, None]).astype(
        jnp.float32
    )
    members = anode_drive.shape[0]
    onehot = (jnp.arange(members, dtype=jnp.int32)[:, None, None] == member[None]).astype(
        jnp.float32
    )
    member_drive = jnp.sum(onehot * anode_drive[:, None, None], axis=0)
    diagonal = self_coef[:, None, :]
    current = exch_current[:, None, :]
    conduct = conductance[:, None, :]

    def near_field(field):
        own_patch = lax.all_gather(field, "col", axis=0, tiled=True)
        before = from_behind(field, "patch", 1)
        following = from_behind(field, "patch", -1)
        stacked = jnp.concatenate([own_patch, before, following], axis=0)
        sources = stacked[pair_source]
        return jnp.einsum(
            "bkij,bkcj->bci",
            nearfield,
            sources * live_mask[:, :, None, None],
            precision=lax.Precision.HIGHEST,
        )

    def mismatch(field, near_value):
        grow = jnp.exp(ALPHA * field)
        shrink = jnp.exp(-BETA * field)
        value = (
            diagonal * field
            + near_value
            + current * (grow - shrink)
            + conduct * (field - member_drive[:, None, :])
            - source_term
        )
        slope = current * (ALPHA * grow + BETA * shrink) + conduct
        return (value, slope)

    field = potential0
    near_now = near_field(field)
    for newton in range(NEWTON):
        value, slope = mismatch(field, near_now)
        start = -value
        beta = jnp.sqrt(lax.psum(column_sum(start, start), ("patch", "col")) + EPS)
        basis = [start / beta[None, :, None]]
        directions = []
        near_images = []
        columns = []
        for step in range(GMRES):
            direction = jnp.einsum(
                "bij,bcj->bci", precond, basis[step], precision=lax.Precision.HIGHEST
            )
            directions.append(direction)
            near_image = near_field(direction)
            near_images.append(near_image)
            image = diagonal * direction + near_image + slope * direction
            coeffs = []
            for place in range(step + 1):
                coeff = lax.psum(column_sum(basis[place], image), ("patch", "col"))
                image = image - coeff[None, :, None] * basis[place]
                coeffs.append(coeff)
            norm = jnp.sqrt(lax.psum(column_sum(image, image), ("patch", "col")) + EPS)
            basis.append(image / norm[None, :, None])
            columns.append(jnp.stack(coeffs + [norm]))
        weights = least_squares(columns, beta)
        update = jnp.zeros_like(field)
        for step in range(GMRES):
            update = update + weights[:, step][None, :, None] * directions[step]
        field = field + update
        near_now = near_field(field)
    final_value, final_slope = mismatch(field, near_now)
    return (field, final_value)


def solution(mesh):
    return jax.shard_map(
        body,
        mesh=mesh,
        in_specs=(
            P(("patch", "col"), None, None),
            P(("patch", "col"), None, None),
            P(("patch", "col"), None),
            P(("patch", "col"), None, None, None),
            P(("patch", "col"), None, None),
            P(("patch", "col"), None),
            P(("patch", "col"), None),
            P(("patch", "col"), None),
            P(),
            P(("patch", "col"), None),
            P(("patch", "col")),
        ),
        out_specs=(P(("patch", "col"), None, None), P(("patch", "col"), None, None)),
        check_vma=False,
    )
```

profile of v0, /device:TPU:1, one launch (start us, length us, event | category | flops | bytes accessed | tf_op | source)
XLA Modules:
  0.0 974.0 jit_solution(4111155873102971596)
XLA Ops:
  0.7 2.1 collective-permute-start
  2.8 3.8 collective-permute-start.1
  6.6 15.1 %all_gather.21 = f32[32,16,128]{2,1,0:T(8,128)S(1)} all-gather(f32[4,16,128]{2,1,0:T(8,128)} %param.24), channel_id=1, replica_groups=mesh['patch'=16,'col'=8] {'col'}, dimensions={0}, use_global_device_ids=true | all-gather | bytes 294912 | tf_op jit(solution)/shard_map/all_gather | solution.py:61
  22.5 0.7 fusion.40
  23.2 0.8 select_reduce_fusion
  24.0 0.7 gather_fusion
  24.7 7.6 multiply_reduce_fusion.11
  32.3 64.2 %psum.84 = f32[16]{0:T(128)S(1)} all-reduce(f32[16]{0:T(128)S(1)} %get-tuple-element.61), channel_id=1, replica_groups=mesh['patch'=16,'col'=8] {'patch','col'}, use_global_device_ids=true, to_apply=%region_2.0 | all-reduce | flops 16 | bytes 128 | tf_op jit(solution)/shard_map/psum | solution.py:91
  97.3 4.6 collective-permute-start.3
  101.9 13.9 %all_gather.22 = f32[32,16,128]{2,1,0:T(8,128)S(1)} all-gather(f32[4,16,128]{2,1,0:T(8,128)S(1)} %fusion.43), channel_id=1, replica_groups=mesh['patch'=16,'col'=8] {'col'}, dimensions={0}, use_global_device_ids=true | all-gather | bytes 294912 | tf_op jit(solution)/shard_map/all_gather | solution.py:61
  115.8 0.7 gather_fusion.1
  116.5 7.5 multiply_reduce_fusion.10
  124.0 63.4 %psum.85 = f32[16]{0:T(128)S(1)} all-reduce(f32[16]{0:T(128)S(1)} %get-tuple-element.63), channel_id=1, replica_groups=mesh['patch'=16,'col'=8] {'patch','col'}, use_global_device_ids=true, to_apply=%region_4.0 | all-reduce | flops 16 | bytes 128 | tf_op jit(solution)/shard_map/psum | solution.py:106
  187.6 63.0 %psum.86 = f32[16]{0:T(128)S(1)} all-reduce(f32[16]{0:T(128)S(1)} %multiply_reduce_fusion.9), channel_id=1, replica_groups=mesh['patch'=16,'col'=8] {'patch','col'}, use_global_device_ids=true, to_apply=%region_6.0 | all-reduce | flops 16 | bytes 128 | tf_op jit(solution)/shard_map/psum | solution.py:109
  251.2 0.8 collective-permute-start.4
  252.1 4.0 collective-permute-start.5
  256.0 13.8 %all_gather.23 = f32[32,16,128]{2,1,0:T(8,128)S(1)} all-gather(f32[4,16,128]{2,1,0:T(8,128)S(1)} %fusion.44), channel_id=1, replica_groups=mesh['patch'=16,'col'=8] {'col'}, dimensions={0}, use_global_device_ids=true | all-gather | bytes 294912 | tf_op jit(solution)/shard_map/all_gather | solution.py:61
  269.8 0.7 gather_fusion.2
  270.5 7.5 multiply_reduce_fusion.8
  278.0 64.4 %psum.87 = f32[16]{0:T(128)S(1)} all-reduce(f32[16]{0:T(128)S(1)} %get-tuple-element.65), channel_id=1, replica_groups=mesh['patch'=16,'col'=8] {'patch','col'}, use_global_device_ids=true, to_apply=%region_8.0 | all-reduce | flops 16 | bytes 128 | tf_op jit(solution)/shard_map/psum | solution.py:106
  342.6 62.5 %psum.88 = f32[16]{0:T(128)S(1)} all-reduce(f32[16]{0:T(128)S(1)} %multiply_reduce_fusion.7), channel_id=1, replica_groups=mesh['patch'=16,'col'=8] {'patch','col'}, use_global_device_ids=true, to_apply=%region_10.0 | all-reduce | flops 16 | bytes 128 | tf_op jit(solution)/shard_map/psum | solution.py:106
  405.3 64.0 %psum.89 = f32[16]{0:T(128)S(1)} all-reduce(f32[16]{0:T(128)S(1)} %multiply_reduce_fusion.6), channel_id=1, replica_groups=mesh['patch'=16,'col'=8] {'patch','col'}, use_global_device_ids=true, to_apply=%region_12.0 | all-reduce | flops 16 | bytes 128 | tf_op jit(solution)/shard_map/psum | solution.py:109
  470.0 3.1 custom-call.12
  473.3 3.0 custom-call.14
  476.7 4.8 collective-permute-start.7
  481.5 14.5 %all_gather.24 = f32[32,16,128]{2,1,0:T(8,128)S(1)} all-gather(f32[4,16,128]{2,1,0:T(8,128)S(1)} %add_add_fusion.1), channel_id=1, replica_groups=mesh['patch'=16,'col'=8] {'col'}, dimensions={0}, use_global_device_ids=true | all-gather | bytes 294912 | tf_op jit(solution)/shard_map/all_gather | solution.py:61
  496.7 7.5 multiply_reduce_fusion.5
  504.2 61.8 %psum.90 = f32[16]{0:T(128)S(1)} all-reduce(f32[16]{0:T(128)S(1)} %get-tuple-element.67), channel_id=1, replica_groups=mesh['patch'=16,'col'=8] {'patch','col'}, use_global_device_ids=true, to_apply=%region_16.0 | all-reduce | flops 16 | bytes 128 | tf_op jit(solution)/shard_map/psum | solution.py:91
  566.6 1.2 collective-permute-start.8
  567.7 3.7 collective-permute-start.9
  571.4 13.9 %all_gather.25 = f32[32,16,128]{2,1,0:T(8,128)S(1)} all-gather(f32[4,16,128]{2,1,0:T(8,128)S(1)} %fusion.45), channel_id=1, replica_groups=mesh['patch'=16,'col'=8] {'col'}, dimensions={0}, use_global_device_ids=true | all-gather | bytes 294912 | tf_op jit(solution)/shard_map/all_gather | solution.py:61
  585.3 0.7 gather_fusion.4
  586.0 7.5 multiply_reduce_fusion.4
  593.5 63.5 %psum.91 = f32[16]{0:T(128)S(1)} all-reduce(f32[16]{0:T(128)S(1)} %get-tuple-element.69), channel_id=1, replica_groups=mesh['patch'=16,'col'=8] {'patch','col'}, use_global_device_ids=true, to_apply=%region_18.0 | all-reduce | flops 16 | bytes 128 | tf_op jit(solution)/shard_map/psum | solution.py:106
  657.1 62.6 %psum.92 = f32[16]{0:T(128)S(1)} all-reduce(f32[16]{0:T(128)S(1)} %multiply_reduce_fusion.3), channel_id=1, replica_groups=mesh['patch'=16,'col'=8] {'patch','col'}, use_global_device_ids=true, to_apply=%region_20.0 | all-reduce | flops 16 | bytes 128 | tf_op jit(solution)/shard_map/psum | solution.py:109
  720.2 0.8 collective-permute-start.10
  721.1 4.0 collective-permute-start.11
  725.0 14.0 %all_gather.26 = f32[32,16,128]{2,1,0:T(8,128)S(1)} all-gather(f32[4,16,128]{2,1,0:T(8,128)S(1)} %fusion.46), channel_id=1, replica_groups=mesh['patch'=16,'col'=8] {'col'}, dimensions={0}, use_global_device_ids=true | all-gather | bytes 294912 | tf_op jit(solution)/shard_map/all_gather | solution.py:61
  739.1 0.7 gather_fusion.5
  739.8 7.5 multiply_reduce_fusion.2
  747.2 64.4 %psum.93 = f32[16]{0:T(128)S(1)} all-reduce(f32[16]{0:T(128)S(1)} %get-tuple-element.71), channel_id=1, replica_groups=mesh['patch'=16,'col'=8] {'patch','col'}, use_global_device_ids=true, to_apply=%region_22.0 | all-reduce | flops 16 | bytes 128 | tf_op jit(solution)/shard_map/psum | solution.py:106
  811.8 62.5 %psum.94 = f32[16]{0:T(128)S(1)} all-reduce(f32[16]{0:T(128)S(1)} %multiply_reduce_fusion.1), channel_id=1, replica_groups=mesh['patch'=16,'col'=8] {'patch','col'}, use_global_device_ids=true, to_apply=%region_24.0 | all-reduce | flops 16 | bytes 128 | tf_op jit(solution)/shard_map/psum | solution.py:106
  874.5 64.0 %psum.95 = f32[16]{0:T(128)S(1)} all-reduce(f32[16]{0:T(128)S(1)} %multiply_reduce_fusion), channel_id=1, replica_groups=mesh['patch'=16,'col'=8] {'patch','col'}, use_global_device_ids=true, to_apply=%region_26.0 | all-reduce | flops 16 | bytes 128 | tf_op jit(solution)/shard_map/psum | solution.py:109
  939.2 3.1 custom-call.15
  942.6 3.0 custom-call.17
  946.0 4.8 collective-permute-start.13
  950.8 14.3 %all_gather.27 = f32[32,16,128]{2,1,0:T(8,128)S(1)} all-gather(f32[4,16,128]{2,1,0:T(8,128)S(1)} %add_add_fusion), channel_id=1, replica_groups=mesh['patch'=16,'col'=8] {'col'}, dimensions={0}, use_global_device_ids=true | all-gather | bytes 294912 | tf_op jit(solution)/shard_map/all_gather | solution.py:61
  965.8 8.0 fusion.3
  (99 shorter events, 8.5 us)
Async XLA Ops:
  0.6 95.9 %copy-start = (f32[4,128,128]{2,1,0:T(8,128)S(1)}, f32[4,128,128]{2,1,0:T(8,128)}, u32[]{:S(2)}) copy-start(f32[4,128,128]{2,1,0:T(8,128)} %param.28) | copy-start | bytes 786436
  0.6 115.9 %copy-start.1 = (f32[4,16,128]{2,1,0:T(8,128)S(1)}, f32[4,16,128]{2,1,0:T(8,128)}, u32[]{:S(2)}) copy-start(f32[4,16,128]{2,1,0:T(8,128)} %param.24) | copy-start | bytes 98308
  0.7 115.9 %copy-start.6 = (f32[4,128]{1,0:T(4,128)S(1)}, f32[4,128]{1,0:T(4,128)}, u32[]{:S(2)}) copy-start(f32[4,128]{1,0:T(4,128)} %param.26) | copy-start | bytes 6148
  0.7 115.9 %copy-start.5 = (f32[4,128]{1,0:T(4,128)S(1)}, f32[4,128]{1,0:T(4,128)}, u32[]{:S(2)}) copy-start(f32[4,128]{1,0:T(4,128)} %param.29) | copy-start | bytes 6148
  0.7 115.9 %copy-start.4 = (f32[4,128]{1,0:T(4,128)S(1)}, f32[4,128]{1,0:T(4,128)}, u32[]{:S(2)}) copy-start(f32[4,128]{1,0:T(4,128)} %param.30) | copy-start | bytes 6148
  0.7 23.3 %collective-permute-start = (f32[4,16,128]{2,1,0:T(8,128)}, f32[4,16,128]{2,1,0:T(8,128)S(1)}, u32[]{:S(2)}, u32[]{:S(2)}) collective-permute-start(f32[4,16,128]{2,1,0:T(8,128)} %param.24), channel_id=1, source_target_pairs={{0,8},{8,16},{16,24},{24,32},{32,40},{40,48},{48,56},{56,64},{64,7... | collective-permute-start | bytes 98312 | tf_op jit(solution)/shard_map/ppermute | solution.py:15
  2.8 21.2 %collective-permute-start.1 = (f32[4,16,128]{2,1,0:T(8,128)}, f32[4,16,128]{2,1,0:T(8,128)S(1)}, u32[]{:S(2)}, u32[]{:S(2)}) collective-permute-start(f32[4,16,128]{2,1,0:T(8,128)} %param.24), channel_id=1, source_target_pairs={{0,120},{8,0},{16,8},{24,16},{32,24},{40,32},{48,40},{56,48},{64,5... | collective-permute-start | bytes 98312 | tf_op jit(solution)/shard_map/ppermute | solution.py:15
  97.1 18.7 %collective-permute-start.2 = (f32[4,16,128]{2,1,0:T(8,128)S(1)}, f32[4,16,128]{2,1,0:T(8,128)S(1)}, u32[]{:S(2)}, u32[]{:S(2)}) collective-permute-start(f32[4,16,128]{2,1,0:T(8,128)S(1)} %fusion.43), channel_id=1, source_target_pairs={{0,8},{8,16},{16,24},{24,32},{32,40},{40,48},{48,56},{56,64},{64,7... | collective-permute-start | bytes 98312 | tf_op jit(solution)/shard_map/ppermute | solution.py:15
  97.3 18.4 %collective-permute-start.3 = (f32[4,16,128]{2,1,0:T(8,128)S(1)}, f32[4,16,128]{2,1,0:T(8,128)S(1)}, u32[]{:S(2)}, u32[]{:S(2)}) collective-permute-start(f32[4,16,128]{2,1,0:T(8,128)S(1)} %fusion.43), channel_id=1, source_target_pairs={{0,120},{8,0},{16,8},{24,16},{32,24},{40,32},{48,40},{56,48},{64,5... | collective-permute-start | bytes 98312 | tf_op jit(solution)/shard_map/ppermute | solution.py:15
  251.2 18.6 %collective-permute-start.4 = (f32[4,16,128]{2,1,0:T(8,128)S(1)}, f32[4,16,128]{2,1,0:T(8,128)S(1)}, u32[]{:S(2)}, u32[]{:S(2)}) collective-permute-start(f32[4,16,128]{2,1,0:T(8,128)S(1)} %fusion.44), channel_id=1, source_target_pairs={{0,8},{8,16},{16,24},{24,32},{32,40},{40,48},{48,56},{56,64},{64,7... | collective-permute-start | bytes 98312 | tf_op jit(solution)/shard_map/ppermute | solution.py:15
  252.1 17.7 %collective-permute-start.5 = (f32[4,16,128]{2,1,0:T(8,128)S(1)}, f32[4,16,128]{2,1,0:T(8,128)S(1)}, u32[]{:S(2)}, u32[]{:S(2)}) collective-permute-start(f32[4,16,128]{2,1,0:T(8,128)S(1)} %fusion.44), channel_id=1, source_target_pairs={{0,120},{8,0},{16,8},{24,16},{32,24},{40,32},{48,40},{56,48},{64,5... | collective-permute-start | bytes 98312 | tf_op jit(solution)/shard_map/ppermute | solution.py:15
  269.8 226.9 %copy-start.2 = (f32[4,16,128]{2,1,0:T(8,128)S(1)}, f32[4,16,128]{2,1,0:T(8,128)}, u32[]{:S(2)}) copy-start(f32[4,16,128]{2,1,0:T(8,128)} %param.25) | copy-start | bytes 98308
  476.7 19.3 %collective-permute-start.6 = (f32[4,16,128]{2,1,0:T(8,128)S(1)}, f32[4,16,128]{2,1,0:T(8,128)S(1)}, u32[]{:S(2)}, u32[]{:S(2)}) collective-permute-start(f32[4,16,128]{2,1,0:T(8,128)S(1)} %add_add_fusion.1), channel_id=1, source_target_pairs={{0,8},{8,16},{16,24},{24,32},{32,40},{40,48},{48,56},{56,64},{64,7... | collective-permute-start | bytes 98312 | tf_op jit(solution)/shard_map/ppermute | solution.py:15
  476.7 19.3 %collective-permute-start.7 = (f32[4,16,128]{2,1,0:T(8,128)S(1)}, f32[4,16,128]{2,1,0:T(8,128)S(1)}, u32[]{:S(2)}, u32[]{:S(2)}) collective-permute-start(f32[4,16,128]{2,1,0:T(8,128)S(1)} %add_add_fusion.1), channel_id=1, source_target_pairs={{0,120},{8,0},{16,8},{24,16},{32,24},{40,32},{48,40},{56,48},{64,5... | collective-permute-start | bytes 98312 | tf_op jit(solution)/shard_map/ppermute | solution.py:15
  566.6 18.7 %collective-permute-start.8 = (f32[4,16,128]{2,1,0:T(8,128)S(1)}, f32[4,16,128]{2,1,0:T(8,128)S(1)}, u32[]{:S(2)}, u32[]{:S(2)}) collective-permute-start(f32[4,16,128]{2,1,0:T(8,128)S(1)} %fusion.45), channel_id=1, source_target_pairs={{0,8},{8,16},{16,24},{24,32},{32,40},{40,48},{48,56},{56,64},{64,7... | collective-permute-start | bytes 98312 | tf_op jit(solution)/shard_map/ppermute | solution.py:15
  567.7 17.5 %collective-permute-start.9 = (f32[4,16,128]{2,1,0:T(8,128)S(1)}, f32[4,16,128]{2,1,0:T(8,128)S(1)}, u32[]{:S(2)}, u32[]{:S(2)}) collective-permute-start(f32[4,16,128]{2,1,0:T(8,128)S(1)} %fusion.45), channel_id=1, source_target_pairs={{0,120},{8,0},{16,8},{24,16},{32,24},{40,32},{48,40},{56,48},{64,5... | collective-permute-start | bytes 98312 | tf_op jit(solution)/shard_map/ppermute | solution.py:15
  720.2 18.8 %collective-permute-start.10 = (f32[4,16,128]{2,1,0:T(8,128)S(1)}, f32[4,16,128]{2,1,0:T(8,128)S(1)}, u32[]{:S(2)}, u32[]{:S(2)}) collective-permute-start(f32[4,16,128]{2,1,0:T(8,128)S(1)} %fusion.46), channel_id=1, source_target_pairs={{0,8},{8,16},{16,24},{24,32},{32,40},{40,48},{48,56},{56,64},{64,7... | collective-permute-start | bytes 98312 | tf_op jit(solution)/shard_map/ppermute | solution.py:15
  721.1 17.9 %collective-permute-start.11 = (f32[4,16,128]{2,1,0:T(8,128)S(1)}, f32[4,16,128]{2,1,0:T(8,128)S(1)}, u32[]{:S(2)}, u32[]{:S(2)}) collective-permute-start(f32[4,16,128]{2,1,0:T(8,128)S(1)} %fusion.46), channel_id=1, source_target_pairs={{0,120},{8,0},{16,8},{24,16},{32,24},{40,32},{48,40},{56,48},{64,5... | collective-permute-start | bytes 98312 | tf_op jit(solution)/shard_map/ppermute | solution.py:15
  945.9 27.9 %copy-start.3 = (f32[4,16,128]{2,1,0:T(8,128)}, f32[4,16,128]{2,1,0:T(8,128)S(1)}, u32[]{:S(2)}) copy-start(f32[4,16,128]{2,1,0:T(8,128)S(1)} %add_add_fusion) | copy-start | bytes 98308
  945.9 19.2 %collective-permute-start.12 = (f32[4,16,128]{2,1,0:T(8,128)S(1)}, f32[4,16,128]{2,1,0:T(8,128)S(1)}, u32[]{:S(2)}, u32[]{:S(2)}) collective-permute-start(f32[4,16,128]{2,1,0:T(8,128)S(1)} %add_add_fusion), channel_id=1, source_target_pairs={{0,8},{8,16},{16,24},{24,32},{32,40},{40,48},{48,56},{56,64},{64,7... | collective-permute-start | bytes 98312 | tf_op jit(solution)/shard_map/ppermute | solution.py:15
  946.0 19.1 %collective-permute-start.13 = (f32[4,16,128]{2,1,0:T(8,128)S(1)}, f32[4,16,128]{2,1,0:T(8,128)S(1)}, u32[]{:S(2)}, u32[]{:S(2)}) collective-permute-start(f32[4,16,128]{2,1,0:T(8,128)S(1)} %add_add_fusion), channel_id=1, source_target_pairs={{0,120},{8,0},{16,8},{24,16},{32,24},{40,32},{48,40},{56,48},{64,5... | collective-permute-start | bytes 98312 | tf_op jit(solution)/shard_map/ppermute | solution.py:15
where the time goes:
time: 984 us; the launch traced here: 974 us
  blocking collectives  860 us (87%)
  matrix products  55.7 us (6%)
  starting transfers between devices  34.8 us (4%)
  other arithmetic  16.5 us (2%)
    psum x6, blocking collectives, body(): coeff = lax.psum(column_sum(basis[place], image), ('patch', 'col'))  381 us
    psum x4, blocking collectives, body(): norm = jnp.sqrt(lax.psum(column_sum(image, image), ('patch', 'col')) + EPS)  254 us
    psum x2, blocking collectives, body(): beta = jnp.sqrt(lax.psum(column_sum(start, start), ('patch', 'col')) + EPS)  126 us
    all_gather x7, blocking collectives, near_field(): own_patch = lax.all_gather(field, 'col', axis=0, tiled=True)  99.4 us
    dot_general x7, matrix products, near_field(): jnp.einsum('bkij,bkcj->bci', nearfield, sources * live_mask[:, :, None, N...  52.9 us
    ppermute x14, starting transfers between devices, from_behind(): lax.ppermute(array, axis, [(i, (i + by) % size) for i in range(size)])  34.8 us
  transfers between devices with their start and end apart: 14, of which 0 were waited for; matrix products, arithmetic and copies ran while one was open for 0% of the time, Pallas kernels for 0%

commit v1 on v0

--- a/solution.py
+++ b/solution.py
@@ -8,6 +8,28 @@
 ALPHA = 0.6
 BETA = 0.4
 EPS = 1e-06
+
+
+def laid_out(blocks, dim):
+    blocks = jnp.moveaxis(blocks, 0, dim)
+    shape = blocks.shape
+    return blocks.reshape(*shape[:dim], shape[dim] * shape[dim + 1], *shape[dim + 2 :])
+
+
+def ring_gather(shard, axis, dim):
+    peers = lax.axis_size(axis)
+    pairs = [(i, (i + 1) % peers) for i in range(peers)]
+    back = [(b, a) for a, b in pairs]
+    lower, upper = ([], [])
+    for step in range(peers - 1):
+        if step % 2 == 0:
+            lower.append(lax.ppermute(lower[-1] if lower else shard, axis, pairs))
+        else:
+            upper.append(lax.ppermute(upper[-1] if upper else shard, axis, back))
+    blocks = jnp.stack([*lower[::-1], shard, *upper])
+    shift = lax.axis_index(axis) - len(lower)
+    blocks = blocks[(jnp.arange(peers) - shift) % peers]
+    return laid_out(blocks, dim)
 
 
 def from_behind(array, axis, by):
@@ -58,7 +80,7 @@
     conduct = conductance[:, None, :]
 
     def near_field(field):
-        own_patch = lax.all_gather(field, "col", axis=0, tiled=True)
+        own_patch = ring_gather(field, "col", 0)
         before = from_behind(field, "patch", 1)
         following = from_behind(field, "patch", -1)
         stacked = jnp.concatenate([own_patch, before, following], axis=0)

time: 984 us -> 1020 us (1.037)
  starting transfers between devices: 34.8 us -> 121 us
  blocking collectives: 860 us -> 782 us
  waiting for transfers between devices: 0.04 us -> 22.6 us
    all_gather x7 -> x0, blocking collectives: 99.4 us -> none  [near_field(): own_patch = lax.all_gather(field, 'col', axis=0, tiled=True)]
    ppermute x0 -> x49, starting transfers between devices: none -> 86.9 us  [the longest x21 43.9 us: ring_gather(): upper.append(lax.ppermute(upper[-1] if upper else shard, axis, back))]
    ppermute x0 -> x49, waiting for transfers between devices: none -> 22.6 us  [the longest x28 17.7 us: ring_gather(): lower.append(lax.ppermute(lower[-1] if lower else shard, axis, pairs))]
    psum x6, blocking collectives: 381 us -> 396 us  [body(): coeff = lax.psum(column_sum(basis[place], image), ('patch', 'col'))]
  transfers between devices with their start and end apart: 14 -> 63, of which waited for: 0 -> 28; matrix products, arithmetic and copies ran while one was open for 0% -> 1% of each run, Pallas kernels for 0% -> 0%
where the time goes in v1:
time: 1020 us; the launch traced here: 1010 us
  blocking collectives  782 us (77%)
  starting transfers between devices  121 us (12%)
  matrix products  55.7 us (5%)
  waiting for transfers between devices  22.6 us (2%)
  other arithmetic  16.5 us (2%)
  local copies, waits for them, and re-layouts  11.1 us (1%)
    psum x6, blocking collectives, body(): coeff = lax.psum(column_sum(basis[place], image), ('patch', 'col'))  396 us
    psum x4, blocking collectives, body(): norm = jnp.sqrt(lax.psum(column_sum(image, image), ('patch', 'col')) + EPS)  252 us
    psum x2, blocking collectives, body(): beta = jnp.sqrt(lax.psum(column_sum(start, start), ('patch', 'col')) + EPS)  135 us
    dot_general x7, matrix products, near_field(): jnp.einsum('bkij,bkcj->bci', nearfield, sources * live_mask[:, :, None, N...  52.9 us
    ppermute x21, starting transfers between devices, ring_gather(): upper.append(lax.ppermute(upper[-1] if upper else shard, axis, back))  43.9 us
    ppermute x28, starting transfers between devices, ring_gather(): lower.append(lax.ppermute(lower[-1] if lower else shard, axis, pairs))  43 us
    ppermute x14, starting transfers between devices, from_behind(): lax.ppermute(array, axis, [(i, (i + by) % size) for i in range(size)])  34.1 us
  transfers between devices with their start and end apart: 63, of which 28 were waited for; matrix products, arithmetic and copies ran while one was open for 1% of the time, Pallas kernels for 0%

profile of v1, /device:TPU:1, one launch (start us, length us, event | category | flops | bytes accessed | tf_op | source)
XLA Modules:
  0.0 1010.6 jit_solution(12729677427613916824)
XLA Ops:
  0.6 3.0 collective-permute-start
  4.9 3.7 collective-permute-start.8
  14.0 2.3 collective-permute-start.2
  19.8 2.7 collective-permute-start.6
  25.3 7.6 multiply_reduce_fusion.11
  32.8 67.3 %psum.84 = f32[16]{0:T(128)S(1)} all-reduce(f32[16]{0:T(128)S(1)} %get-tuple-element.61), channel_id=1, replica_groups=mesh['patch'=16,'col'=8] {'patch','col'}, use_global_device_ids=true, to_apply=%region_2.3 | all-reduce | flops 16 | bytes 128 | tf_op jit(solution)/shard_map/psum | solution.py:113
  102.7 2.3 collective-permute-start.10
  111.7 4.8 collective-permute-start.17
  116.5 3.8 collective-permute-start.15
  122.5 7.5 multiply_reduce_fusion.10
  130.0 67.3 %psum.85 = f32[16]{0:T(128)S(1)} all-reduce(f32[16]{0:T(128)S(1)} %get-tuple-element.63), channel_id=1, replica_groups=mesh['patch'=16,'col'=8] {'patch','col'}, use_global_device_ids=true, to_apply=%region_4.5 | all-reduce | flops 16 | bytes 128 | tf_op jit(solution)/shard_map/psum | solution.py:128
  197.5 62.6 %psum.86 = f32[16]{0:T(128)S(1)} all-reduce(f32[16]{0:T(128)S(1)} %multiply_reduce_fusion.9), channel_id=1, replica_groups=mesh['patch'=16,'col'=8] {'patch','col'}, use_global_device_ids=true, to_apply=%region_6.7 | all-reduce | flops 16 | bytes 128 | tf_op jit(solution)/shard_map/psum | solution.py:131
  263.3 2.3 collective-permute-start.19
  266.7 2.3 collective-permute-start.20
  272.8 4.8 collective-permute-start.26
  277.6 3.2 collective-permute-start.24
  283.0 7.5 multiply_reduce_fusion.8
  290.5 67.2 %psum.87 = f32[16]{0:T(128)S(1)} all-reduce(f32[16]{0:T(128)S(1)} %get-tuple-element.65), channel_id=1, replica_groups=mesh['patch'=16,'col'=8] {'patch','col'}, use_global_device_ids=true, to_apply=%region_8.9 | all-reduce | flops 16 | bytes 128 | tf_op jit(solution)/shard_map/psum | solution.py:128
  357.8 63.5 %psum.88 = f32[16]{0:T(128)S(1)} all-reduce(f32[16]{0:T(128)S(1)} %multiply_reduce_fusion.7), channel_id=1, replica_groups=mesh['patch'=16,'col'=8] {'patch','col'}, use_global_device_ids=true, to_apply=%region_10.11 | all-reduce | flops 16 | bytes 128 | tf_op jit(solution)/shard_map/psum | solution.py:128
  421.6 62.7 %psum.89 = f32[16]{0:T(128)S(1)} all-reduce(f32[16]{0:T(128)S(1)} %multiply_reduce_fusion.6), channel_id=1, replica_groups=mesh['patch'=16,'col'=8] {'patch','col'}, use_global_device_ids=true, to_apply=%region_12.13 | all-reduce | flops 16 | bytes 128 | tf_op jit(solution)/shard_map/psum | solution.py:131
  484.9 3.1 custom-call.12
  488.3 3.0 custom-call.14
  494.2 2.3 collective-permute-start.28
  497.5 2.3 collective-permute-start.29
  503.2 4.8 collective-permute-start.35
  508.0 3.3 collective-permute-start.33
  513.4 7.5 multiply_reduce_fusion.5
  520.9 67.4 %psum.90 = f32[16]{0:T(128)S(1)} all-reduce(f32[16]{0:T(128)S(1)} %get-tuple-element.67), channel_id=1, replica_groups=mesh['patch'=16,'col'=8] {'patch','col'}, use_global_device_ids=true, to_apply=%region_16.20 | all-reduce | flops 16 | bytes 128 | tf_op jit(solution)/shard_map/psum | solution.py:113
  596.0 2.8 collective-permute-start.41
  599.8 4.6 collective-permute-start.44
  604.3 4.4 collective-permute-start.42
  610.9 7.5 multiply_reduce_fusion.4
  618.4 67.3 %psum.91 = f32[16]{0:T(128)S(1)} all-reduce(f32[16]{0:T(128)S(1)} %get-tuple-element.69), channel_id=1, replica_groups=mesh['patch'=16,'col'=8] {'patch','col'}, use_global_device_ids=true, to_apply=%region_18.22 | all-reduce | flops 16 | bytes 128 | tf_op jit(solution)/shard_map/psum | solution.py:128
  685.9 62.5 %psum.92 = f32[16]{0:T(128)S(1)} all-reduce(f32[16]{0:T(128)S(1)} %multiply_reduce_fusion.3), channel_id=1, replica_groups=mesh['patch'=16,'col'=8] {'patch','col'}, use_global_device_ids=true, to_apply=%region_20.24 | all-reduce | flops 16 | bytes 128 | tf_op jit(solution)/shard_map/psum | solution.py:131
  751.6 2.3 collective-permute-start.46
  755.0 2.3 collective-permute-start.47
  760.6 4.8 collective-permute-start.53
  765.4 3.2 collective-permute-start.51
  770.8 7.5 multiply_reduce_fusion.2
  778.3 67.5 %psum.93 = f32[16]{0:T(128)S(1)} all-reduce(f32[16]{0:T(128)S(1)} %get-tuple-element.71), channel_id=1, replica_groups=mesh['patch'=16,'col'=8] {'patch','col'}, use_global_device_ids=true, to_apply=%region_22.26 | all-reduce | flops 16 | bytes 128 | tf_op jit(solution)/shard_map/psum | solution.py:128
  846.0 62.9 %psum.94 = f32[16]{0:T(128)S(1)} all-reduce(f32[16]{0:T(128)S(1)} %multiply_reduce_fusion.1), channel_id=1, replica_groups=mesh['patch'=16,'col'=8] {'patch','col'}, use_global_device_ids=true, to_apply=%region_24.28 | all-reduce | flops 16 | bytes 128 | tf_op jit(solution)/shard_map/psum | solution.py:128
  909.1 63.8 %psum.95 = f32[16]{0:T(128)S(1)} all-reduce(f32[16]{0:T(128)S(1)} %multiply_reduce_fusion), channel_id=1, replica_groups=mesh['patch'=16,'col'=8] {'patch','col'}, use_global_device_ids=true, to_apply=%region_26.30 | all-reduce | flops 16 | bytes 128 | tf_op jit(solution)/shard_map/psum | solution.py:131
  973.5 3.1 custom-call.15
  976.9 3.0 custom-call.17
  986.9 3.3 collective-permute-start.59
  991.1 4.7 collective-permute-start.62
  995.8 4.4 collective-permute-start.60
  1002.4 8.0 fusion.3
  (255 shorter events, 76.9 us)
Async XLA Ops:
  0.6 10.2 %collective-permute-start = (f32[4,16,128]{2,1,0:T(8,128)}, f32[4,16,128]{2,1,0:T(8,128)S(1)}, u32[]{:S(2)}, u32[]{:S(2)}) collective-permute-start(f32[4,16,128]{2,1,0:T(8,128)} %param.24), channel_id=1, source_target_pairs={{0,1},{1,2},{2,3},{3,4},{4,5},{5,6},{6,7},{7,0},{8,9},{9,10},{10,1... | collective-permute-start | bytes 98312 | tf_op jit(solution)/shard_map/ppermute | solution.py:26
  3.7 12.8 %collective-permute-start.4 = (f32[4,16,128]{2,1,0:T(8,128)}, f32[4,16,128]{2,1,0:T(8,128)S(1)}, u32[]{:S(2)}, u32[]{:S(2)}) collective-permute-start(f32[4,16,128]{2,1,0:T(8,128)} %param.24), channel_id=1, source_target_pairs={{1,0},{2,1},{3,2},{4,3},{5,4},{6,5},{7,6},{0,7},{9,8},{10,9},{11,1... | collective-permute-start | bytes 98312 | tf_op jit(solution)/shard_map/ppermute | solution.py:28
  3.7 20.8 %collective-permute-start.7 = (f32[4,16,128]{2,1,0:T(8,128)}, f32[4,16,128]{2,1,0:T(8,128)S(1)}, u32[]{:S(2)}, u32[]{:S(2)}) collective-permute-start(f32[4,16,128]{2,1,0:T(8,128)} %param.24), channel_id=1, source_target_pairs={{0,8},{8,16},{16,24},{24,32},{32,40},{40,48},{48,56},{56,64},{64,7... | collective-permute-start | bytes 98312 | tf_op jit(solution)/shard_map/ppermute | solution.py:37
  4.9 19.6 %collective-permute-start.8 = (f32[4,16,128]{2,1,0:T(8,128)}, f32[4,16,128]{2,1,0:T(8,128)S(1)}, u32[]{:S(2)}, u32[]{:S(2)}) collective-permute-start(f32[4,16,128]{2,1,0:T(8,128)} %param.24), channel_id=1, source_target_pairs={{0,120},{8,0},{16,8},{24,16},{32,24},{40,32},{48,40},{56,48},{64,5... | collective-permute-start | bytes 98312 | tf_op jit(solution)/shard_map/ppermute | solution.py:37
  14.0 4.5 collective-permute-start.2
  18.5 4.6 collective-permute-start.3
  19.8 4.1 collective-permute-start.6
  102.7 3.8 collective-permute-start.10
  105.1 3.3 collective-permute-start.13
  106.5 4.6 collective-permute-start.11
  108.4 8.1 collective-permute-start.14
  111.1 9.2 collective-permute-start.12
  111.7 10.0 collective-permute-start.16
  111.7 10.0 collective-permute-start.17
  116.5 4.6 collective-permute-start.15
  265.7 3.4 collective-permute-start.22
  266.7 4.3 collective-permute-start.20
  269.0 8.6 collective-permute-start.23
  271.0 9.7 collective-permute-start.21
  272.3 9.9 collective-permute-start.25
  272.8 9.4 collective-permute-start.26
  277.6 4.1 collective-permute-start.24
  497.5 4.5 collective-permute-start.29
  499.9 8.1 collective-permute-start.32
  502.0 9.2 collective-permute-start.30
  503.2 9.5 collective-permute-start.34
  503.2 9.5 collective-permute-start.35
  508.0 4.1 collective-permute-start.33
  590.5 4.6 collective-permute-start.37
  595.0 4.6 collective-permute-start.38
  596.0 8.3 collective-permute-start.41
  599.6 9.2 collective-permute-start.39
  599.6 10.6 %collective-permute-start.43 = (f32[4,16,128]{2,1,0:T(8,128)S(1)}, f32[4,16,128]{2,1,0:T(8,128)S(1)}, u32[]{:S(2)}, u32[]{:S(2)}) collective-permute-start(f32[4,16,128]{2,1,0:T(8,128)S(1)} %fusion.47), channel_id=1, source_target_pairs={{0,8},{8,16},{16,24},{24,32},{32,40},{40,48},{48,56},{56,64},{64,7... | collective-permute-start | bytes 98312 | tf_op jit(solution)/shard_map/ppermute | solution.py:37
  599.8 10.4 %collective-permute-start.44 = (f32[4,16,128]{2,1,0:T(8,128)S(1)}, f32[4,16,128]{2,1,0:T(8,128)S(1)}, u32[]{:S(2)}, u32[]{:S(2)}) collective-permute-start(f32[4,16,128]{2,1,0:T(8,128)S(1)} %fusion.47), channel_id=1, source_target_pairs={{0,120},{8,0},{16,8},{24,16},{32,24},{40,32},{48,40},{56,48},{64,5... | collective-permute-start | bytes 98312 | tf_op jit(solution)/shard_map/ppermute | solution.py:37
  604.3 5.3 collective-permute-start.42
  755.0 4.4 collective-permute-start.47
  757.3 8.1 collective-permute-start.50
  759.4 9.2 collective-permute-start.48
  760.6 9.4 collective-permute-start.52
  760.6 9.4 collective-permute-start.53
  765.4 4.1 collective-permute-start.51
  981.9 4.5 collective-permute-start.55
  986.4 4.6 collective-permute-start.56
  986.9 8.8 collective-permute-start.59
  991.0 9.2 collective-permute-start.57
  991.0 10.6 %collective-permute-start.61 = (f32[4,16,128]{2,1,0:T(8,128)S(1)}, f32[4,16,128]{2,1,0:T(8,128)S(1)}, u32[]{:S(2)}, u32[]{:S(2)}) collective-permute-start(f32[4,16,128]{2,1,0:T(8,128)S(1)} %add_add_fusion), channel_id=1, source_target_pairs={{0,8},{8,16},{16,24},{24,32},{32,40},{40,48},{48,56},{56,64},{64,7... | collective-permute-start | bytes 98312 | tf_op jit(solution)/shard_map/ppermute | solution.py:37
  991.1 10.6 %collective-permute-start.62 = (f32[4,16,128]{2,1,0:T(8,128)S(1)}, f32[4,16,128]{2,1,0:T(8,128)S(1)}, u32[]{:S(2)}, u32[]{:S(2)}) collective-permute-start(f32[4,16,128]{2,1,0:T(8,128)S(1)} %add_add_fusion), channel_id=1, source_target_pairs={{0,120},{8,0},{16,8},{24,16},{32,24},{40,32},{48,40},{56,48},{64,5... | collective-permute-start | bytes 98312 | tf_op jit(solution)/shard_map/ppermute | solution.py:37
  995.8 5.3 collective-permute-start.60
  (22 other events, 795.8 us)
